TPU v7x, 32 devices: a whole 2x2x4 slice. The times are simulated.
32 devices in a mesh: grp: 2 (over y), freq: 8 (over z, x), site: 2 (over core).
Axes of the slice: x: 2, y: 2, z: 4, core: 2. Of those that a mesh axis runs over, the one named last changes fastest.
Arguments:
- green: bfloat16 [8, 1024, 8, 3, 2, 128], P('freq', None, ('grp', 'site')), parts along dimension 2, may hold values from -0.1875 to 0.1875
- slip: bfloat16 [8, 16, 8, 128], P(None, 'site'), may hold values from 0.099609375 to 1
- positions: float32 [3, 1024], replicated, may hold values from 0 to 40
- hypocenters: float32 [8, 4, 3], replicated, may hold values from 0 to 40
- slowness: float32 [8, 4], replicated, may hold values from 1 to 3
- rise: float32 [8, 16], replicated, may hold values from 0.5 to 6
- block_lists: int32 [8, 8], replicated, may hold values from 0 to 7, as said below
- block_counts: int32 [8], replicated, may hold values from 1 to 8, 48 in all
- var_counts: int32 [8], replicated, may hold values from 1 to 64, as said below
- region_map: int32 [8], replicated, may hold values from 0 to 7, each once
Outputs:
- seismograms: float32 [512, 8, 3, 2048], P('freq', ('grp', 'site')), parts along dimension 1
There are 2 independent parts, one for each index of `grp`. A program takes and returns all parts, laid end to end along the dimension named above; an argument that names none is the same for every part. Nothing has to cross between parts.
Inputs may be any that keep to these rules, and one draw needn't show every extreme that they name: `block_lists`: rupture r lists consecutive blocks s_r, s_r + 1, ... modulo 8; only its first block_counts[r] entries are used. `block_counts`: the counts sum to 48. Variations 0 .. var_counts[r] - 1 of rupture r are live. `region_map`: each row appears once.
All inputs are finite; a program needn't handle non-finite values.
Results may differ from a plain program's by a relative error of at most 0.0048.
Values may be sent and summed in bfloat16 or wider, within the bound.
A program may use at most 192 MiB of HBM per device.

v0:
```python
import math
import jax
import jax.numpy as jnp
from jax import lax
from jax.sharding import PartitionSpec as P

F = 1024
C = 3
TWO_PI = 2.0 * math.pi
OUT_GAIN = 8.0


def on_device(
    green,
    slip,
    positions,
    hypocenters,
    slowness,
    rise,
    block_lists,
    block_counts,
    var_counts,
    region_map,
):
    freq_count = lax.axis_size("freq")
    fdev_bins = green.shape[1] // freq_count
    point_count = green.shape[-1]
    rupture_count = block_lists.shape[0]
    list_len = block_lists.shape[1]
    hypo_count = hypocenters.shape[1]
    wave_len = 2 * F
    slip_all = lax.all_gather(slip, "site", axis=1, tiled=True)
    real_count = slip_all.shape[1]
    first_bin = lax.axis_index("freq") * fdev_bins
    local_bins = first_bin + jnp.arange(fdev_bins, dtype=jnp.int32)
    omegas = TWO_PI * local_bins.astype(jnp.float32) / wave_len
    points_all = positions.reshape(3, positions.shape[1] // point_count, point_count)
    slot_total = rupture_count * list_len
    slot_index = jnp.arange(slot_total, dtype=jnp.int32)
    slot_rup = slot_index // list_len
    slot_pos = slot_index % list_len
    slot_live = slot_pos < block_counts[slot_rup]
    group_size = math.gcd(slot_total, 32)
    turn_count = slot_total // group_size
    rupture_ids = jnp.arange(rupture_count, dtype=jnp.int32)
    tiles_here = lax.all_to_all(green, "freq", split_axis=1, concat_axis=0, tiled=True)
    site_items = tiles_here.shape[2]

    def one_turn(turn_index, totals):
        start = turn_index * group_size
        group_rup = lax.dynamic_slice_in_dim(slot_rup, start, group_size)
        group_pos = lax.dynamic_slice_in_dim(slot_pos, start, group_size)
        group_live = lax.dynamic_slice_in_dim(slot_live, start, group_size)
        blocks = block_lists[group_rup, group_pos]
        tile = tiles_here[region_map[blocks]].astype(jnp.float32)
        points = points_all[:, blocks, :].transpose(1, 0, 2)
        centers = hypocenters[group_rup]
        slows = slowness[group_rup]
        sq_dist = jnp.sum((points[:, None, :, :] - centers[:, :, :, None]) ** 2, axis=2)
        onset_time = slows[:, :, None] * jnp.sqrt(sq_dist)
        phases = omegas[None, None, :, None] * onset_time[:, :, None, :]
        wave_re = jnp.cos(phases)[:, :, :, None, None, :]
        wave_im = -jnp.sin(phases)[:, :, :, None, None, :]
        tile_re = tile[:, None, :, :, :, 0, :]
        tile_im = tile[:, None, :, :, :, 1, :]
        weighted = jnp.stack(
            [wave_re * tile_re - wave_im * tile_im, wave_re * tile_im + wave_im * tile_re], axis=5
        ).astype(jnp.bfloat16)
        amps = slip_all[group_rup, :, group_pos]
        amps = jnp.where(group_live[:, None, None], amps, jnp.zeros_like(amps))
        onehot = (group_rup[None, :] == rupture_ids[:, None]).astype(jnp.bfloat16)
        routed = onehot[:, :, None, None] * amps[None, :, :, :]
        term = jnp.einsum(
            "rgkp,ghfscqp->rkhfscq", routed, weighted, preferred_element_type=jnp.float32
        )
        return totals + term

    start_totals = jnp.zeros(
        (rupture_count, real_count, hypo_count, fdev_bins, site_items, C, 2), jnp.float32
    )
    totals = lax.fori_loop(0, turn_count, one_turn, start_totals)
    ratio = omegas[None, None, :] * rise[:, :, None]
    denom = 1.0 + ratio * ratio
    stf_re = (1.0 / denom)[:, :, None, :, None, None]
    stf_im = (-ratio / denom)[:, :, None, :, None, None]
    part_re = totals[..., 0]
    part_im = totals[..., 1]
    spec_re = stf_re * part_re - stf_im * part_im
    spec_im = stf_re * part_im + stf_im * part_re
    spectrum = jnp.stack([spec_re, spec_im], axis=-1).transpose(0, 1, 2, 4, 5, 6, 3)
    variation = (
        jnp.arange(real_count, dtype=jnp.int32)[:, None] * hypo_count
        + jnp.arange(hypo_count, dtype=jnp.int32)[None, :]
    )
    live = variation[None, :, :] < var_counts[:, None, None]
    spectrum = jnp.where(live[:, :, :, None, None, None, None], spectrum, jnp.zeros_like(spectrum))
    spectrum = spectrum.reshape(
        rupture_count * real_count * hypo_count, site_items, C, 2, fdev_bins
    ).astype(jnp.bfloat16)
    own_rows = lax.all_to_all(spectrum, "freq", split_axis=0, concat_axis=4, tiled=True)
    row_count = own_rows.shape[0]
    site_count = own_rows.shape[1]
    spec_rows = own_rows.reshape(row_count * site_count * C, 2 * F)
    bins = jnp.arange(F, dtype=jnp.int32)
    piece_len = min(512, wave_len)
    pieces = []
    for piece_index in range(wave_len // piece_len):
        samples = piece_index * piece_len + jnp.arange(piece_len, dtype=jnp.int32)
        products = bins[:, None] * samples[None, :] % wave_len
        angles = TWO_PI * products.astype(jnp.float32) / wave_len
        wave_table = jnp.concatenate([jnp.cos(angles), -jnp.sin(angles)], axis=0).astype(
            jnp.bfloat16
        )
        pieces.append(
            jnp.dot(spec_rows, wave_table, preferred_element_type=jnp.float32)
            * (OUT_GAIN / math.sqrt(F))
        )
    motion = jnp.concatenate(pieces, axis=1)
    return motion.reshape(row_count, site_count, C, wave_len)


def solution(mesh):
    placed = (
        P("freq", None, ("grp", "site"), None, None, None),
        P(None, "site", None, None),
        P(),
        P(),
        P(),
        P(),
        P(),
        P(),
        P(),
        P(),
    )
    return jax.shard_map(
        on_device,
        mesh=mesh,
        in_specs=placed,
        out_specs=P("freq", ("grp", "site"), None, None),
        check_vma=False,
    )
```

profile of v0, /device:TPU:0, one launch (start us, length us, event | category | flops | bytes accessed | tf_op | source)
XLA Modules:
  0.0 425.7 jit_solution(9974423023385828386)
XLA Ops:
  0.0 7.4 %all-to-all-start = ((bf16[1,1024,2,3,2,128]{5,4,3,2,0,1:T(2,128)(2,1)}), bf16[1,1024,2,3,2,128]{5,4,3,2,0,1:T(2,128)(2,1)S(1)}, u32[]{:S(2)}, u32[]{:S(2)}) async-start(bf16[1,1024,2,3,2,128]{5,4,3,2,0,1:T(2,128)(2,1)} %bitcast.80), calls=%async_computation | async-start | bytes 6291456 | tf_op jit(solution)/shard_map/all_to_all | solution.py:46
  7.5 0.1 copy.70
  7.7 2.1 all_gather.3
  9.9 0.7 fusion.80
  10.6 5.2 %fusion.75 = pred[64]{0:T(512)(128)(4,1)S(1)} fusion(s32[]{:T(128)} %bitcast.2, s32[]{:T(128)} %bitcast.3, s32[]{:T(128)} %bitcast.4, s32[]{:T(128)} %bitcast.5, s32[]{:T(128)} %bitcast.6, s32[]{:T(128)} %bitcast.8, s32[]{:T(128)} %bitcast.7, s32[]{:T(128)} %bitcast.1), kind=kLoop, calls=%fused_computation.141 | loop fusion | flops 2048 | bytes 96 | tf_op jit(solution)/shard_map/lt | solution.py:42
  15.8 0.7 broadcast_compare_fusion
  16.4 0.7 fusion.73
  17.2 61.0 %all-to-all-done = bf16[1,1024,2,3,2,128]{5,4,3,2,0,1:T(2,128)(2,1)S(1)} async-done(((bf16[1,1024,2,3,2,128]{5,4,3,2,0,1:T(2,128)(2,1)}), bf16[1,1024,2,3,2,128]{5,4,3,2,0,1:T(2,128)(2,1)S(1)}, u32[]{:S(2)}, u32[]{:S(2)}) %all-to-all-start) | async-done | bytes 3145760 | tf_op jit(solution)/shard_map/all_to_all | solution.py:46
  78.2 1.6 copy-done.2
  79.8 2.8 copy.71
  82.7 275.0 %while.14 = (s32[]{:T(128)}, f32[8,16,4,128,2,3,2]{3,1,6,5,4,2,0:T(8,128)}, s32[64]{0:T(128)S(1)}, pred[64]{0:T(512)(128)(4,1)S(1)}, s32[64]{0:T(128)S(1)}, /*in...) while((s32[]{:T(128)}, ...), condition=%wide.region_2.3_spmd.clone, body=%wide.region_0.2_spmd.clone.sunk | while | flops 6658150912 | bytes 280112832 | solution.py:81
  82.8 0.7 gather_fusion.1
  83.5 0.6 gather_fusion.2
  84.2 0.6 gather_fusion
  84.8 0.1 copy.93
  84.9 0.1 multiply_reduce_fusion.2
  85.0 0.6 gather_fusion.3
  85.7 0.1 sqrt_multiply_fusion.2
  85.8 32.0 %multiply_cosine_fusion.2 = (f32[32,4,128,128]{3,2,0,1:T(8,128)}, f32[32,4,128,128]{3,2,0,1:T(8,128)}) fusion(f32[32,4,128]{2,0,1:T(8,128)S(1)} %sqrt_multiply_fusion.2, f32[128]{0:T(128)S(1)} %convert_multiply_fusion.3), kind=kLoop, calls=%fused_computation.16.clone.1 | loop fusion | flops 4194304 | bytes 16843264 | tf_op jit(solution)/shard_map/while/body/eval_jaxpr/cos | solution.py:62
  117.7 0.7 gather_fusion.4
  118.5 6.8 %gather_fusion.5 = bf16[32,128,2,3,2,128]{5,1,4,3,2,0:T(8,128)(2,1)} fusion(bf16[8,128,2,3,2,128]{5,1,4,3,2,0:T(8,128)(2,1)S(1)} %get-tuple-element.556, s32[1024]{0:T(1024)S(1)} %pad_clamp_fusion.8), kind=kCustom, calls=%fused_computation.6.clone.clone.1 | custom fusion | bytes 25165952 | tf_op jit(solution)/shard_map/while/body/eval_jaxpr/gather | solution.py:55
  125.3 14.4 %convert_element_type.116 = f32[32,128,2,3,2,128]{5,1,4,3,2,0:T(8,128)} convert(bf16[32,128,2,3,2,128]{5,1,4,3,2,0:T(8,128)(2,1)} %gather_fusion.5) | non-fusion elementwise | flops 6291456 | bytes 37748736 | tf_op jit(solution)/shard_map/while/body/eval_jaxpr/convert_element_type | solution.py:55
  139.7 14.2 %slice_bitcast_fusion.3 = (f32[32,128,2,3,128]{4,1,3,2,0:T(8,128)S(1)}, f32[32,128,2,3,128]{4,1,3,2,0:T(8,128)}) fusion(f32[32,128,2,3,2,128]{5,1,4,3,2,0:T(8,128)} %convert_element_type.116), kind=kLoop, calls=%fused_computation.14.clone.1 | loop fusion | bytes 50331648 | tf_op jit(solution)/shard_map/while/body/eval_jaxpr/mul | solution.py:67
  153.9 41.2 %subtract_convert_fusion.2 = (bf16[32,4,128,2,3,1,128]{6,2,0,5,4,3,1:T(8,128)(2,1)}, bf16[32,4,128,2,3,1,128]{6,2,0,5,4,3,1:T(8,128)(2,1)}) fusion(f32[32,4,128,128]{3,2,0,1:T(8,128)} %get-tuple-element.505, f32[32,4,128,128]{3,2,0,1:T(8,128)} %get-tuple-element.506, f32[32,128,2,3,128]{4,1,3,2,0:T(8,128)S(1)} %get-tuple-element.507, ...), kind=kLoop, calls=%fused_computation.11.clone.1 | loop fusion | flops 100663296 | bytes 92274688 | tf_op jit(solution)/shard_map/convert
  195.1 1.6 gather_fusion.6
  196.8 0.1 broadcast_select_fusion.2
  196.9 23.2 %bitcast_add_fusion.2 = f32[8,16,4,128,2,3,2]{3,1,6,5,4,2,0:T(8,128)} fusion(f32[8,16,4,128,2,3,2]{3,1,6,5,4,2,0:T(8,128)} %get-tuple-element.529, bf16[32,4,128,2,3,1,128]{6,2,0,5,4,3,1:T(8,128)(2,1)} %get-tuple-element.509, bf16[32,4,128,2,3,1,128]{6,2,0,5,4,3,1:T(8,128)(2,1)} %get-tuple-element.510, pred[]{:T(512)S(6)} %compare.103, ...), kind=kOutput, calls=%fused_computation.18.clone.1 | convolution fusion | flops 6546784256 | bytes 56754688 | tf_op jit(solution)/shard_map/while/body/eval_jaxpr/rgkp,ghfscqp->rkhfscq/dot_general | solution.py:73
  220.2 0.7 gather_fusion.1
  220.9 0.6 gather_fusion.2
  221.5 0.6 gather_fusion
  222.1 0.1 copy.93
  222.2 0.1 multiply_reduce_fusion.2
  222.4 0.6 gather_fusion.3
  223.1 32.0 %multiply_cosine_fusion.2 = (f32[32,4,128,128]{3,2,0,1:T(8,128)}, f32[32,4,128,128]{3,2,0,1:T(8,128)}) fusion(f32[32,4,128]{2,0,1:T(8,128)S(1)} %sqrt_multiply_fusion.2, f32[128]{0:T(128)S(1)} %convert_multiply_fusion.3), kind=kLoop, calls=%fused_computation.16.clone.1 | loop fusion | flops 4194304 | bytes 16843264 | tf_op jit(solution)/shard_map/while/body/eval_jaxpr/cos | solution.py:62
  255.1 0.7 gather_fusion.4
  255.8 6.8 %gather_fusion.5 = bf16[32,128,2,3,2,128]{5,1,4,3,2,0:T(8,128)(2,1)} fusion(bf16[8,128,2,3,2,128]{5,1,4,3,2,0:T(8,128)(2,1)S(1)} %get-tuple-element.556, s32[1024]{0:T(1024)S(1)} %pad_clamp_fusion.8), kind=kCustom, calls=%fused_computation.6.clone.clone.1 | custom fusion | bytes 25165952 | tf_op jit(solution)/shard_map/while/body/eval_jaxpr/gather | solution.py:55
  262.6 14.4 %convert_element_type.116 = f32[32,128,2,3,2,128]{5,1,4,3,2,0:T(8,128)} convert(bf16[32,128,2,3,2,128]{5,1,4,3,2,0:T(8,128)(2,1)} %gather_fusion.5) | non-fusion elementwise | flops 6291456 | bytes 37748736 | tf_op jit(solution)/shard_map/while/body/eval_jaxpr/convert_element_type | solution.py:55
  277.0 14.2 %slice_bitcast_fusion.3 = (f32[32,128,2,3,128]{4,1,3,2,0:T(8,128)S(1)}, f32[32,128,2,3,128]{4,1,3,2,0:T(8,128)}) fusion(f32[32,128,2,3,2,128]{5,1,4,3,2,0:T(8,128)} %convert_element_type.116), kind=kLoop, calls=%fused_computation.14.clone.1 | loop fusion | bytes 50331648 | tf_op jit(solution)/shard_map/while/body/eval_jaxpr/mul | solution.py:67
  291.2 41.2 %subtract_convert_fusion.2 = (bf16[32,4,128,2,3,1,128]{6,2,0,5,4,3,1:T(8,128)(2,1)}, bf16[32,4,128,2,3,1,128]{6,2,0,5,4,3,1:T(8,128)(2,1)}) fusion(f32[32,4,128,128]{3,2,0,1:T(8,128)} %get-tuple-element.505, f32[32,4,128,128]{3,2,0,1:T(8,128)} %get-tuple-element.506, f32[32,128,2,3,128]{4,1,3,2,0:T(8,128)S(1)} %get-tuple-element.507, ...), kind=kLoop, calls=%fused_computation.11.clone.1 | loop fusion | flops 100663296 | bytes 92274688 | tf_op jit(solution)/shard_map/convert
  332.4 1.6 gather_fusion.6
  334.1 0.1 broadcast_select_fusion.2
  334.2 23.5 %bitcast_add_fusion.2 = f32[8,16,4,128,2,3,2]{3,1,6,5,4,2,0:T(8,128)} fusion(f32[8,16,4,128,2,3,2]{3,1,6,5,4,2,0:T(8,128)} %get-tuple-element.529, bf16[32,4,128,2,3,1,128]{6,2,0,5,4,3,1:T(8,128)(2,1)} %get-tuple-element.509, bf16[32,4,128,2,3,1,128]{6,2,0,5,4,3,1:T(8,128)(2,1)} %get-tuple-element.510, pred[]{:T(512)S(6)} %compare.103, ...), kind=kOutput, calls=%fused_computation.18.clone.1 | convolution fusion | flops 6546784256 | bytes 56754688 | tf_op jit(solution)/shard_map/while/body/eval_jaxpr/rgkp,ghfscqp->rkhfscq/dot_general | solution.py:73
  357.7 2.4 multiply_subtract_fusion
  360.1 0.4 fusion.58
  360.5 2.0 copy.72
  362.5 2.8 copy.73
  365.3 3.6 all-to-all-start.1
  368.9 9.3 %negate_convert_fusion.3 = (bf16[1024,512]{1,0:T(8,128)(2,1)}, bf16[1024,512]{1,0:T(8,128)(2,1)}) fusion(), kind=kLoop, calls=%fused_computation.97 | loop fusion | flops 8912896 | bytes 2097152 | tf_op jit(solution)/shard_map/convert.9
  378.2 9.4 %cosine_convert_fusion.1 = (bf16[1024,512]{1,0:T(8,128)(2,1)}, bf16[1024,512]{1,0:T(8,128)(2,1)}) fusion(s32[512]{0:T(512)S(1)} %iota_add_fusion.1), kind=kLoop, calls=%fused_computation.90 | loop fusion | flops 8912896 | bytes 2099200 | tf_op jit(solution)/shard_map/convert.4
  387.6 9.4 %cosine_convert_fusion.2 = (bf16[1024,512]{1,0:T(8,128)(2,1)}, bf16[1024,512]{1,0:T(8,128)(2,1)}) fusion(s32[512]{0:T(512)S(1)} %iota_add_fusion.2), kind=kLoop, calls=%fused_computation.94 | loop fusion | flops 8912896 | bytes 2099200 | tf_op jit(solution)/shard_map/convert.6
  397.0 9.3 %cosine_convert_fusion = (bf16[1024,512]{1,0:T(8,128)(2,1)}, bf16[1024,512]{1,0:T(8,128)(2,1)}) fusion(s32[512]{0:T(512)S(1)} %iota_add_fusion), kind=kLoop, calls=%fused_computation.86 | loop fusion | flops 8912896 | bytes 2099200 | tf_op jit(solution)/shard_map/convert.2
  406.3 1.8 copy.85
  408.2 0.7 reshape.209
  408.9 2.7 fusion.62
  411.6 1.0 fusion.65
  412.6 0.2 copy-done.8
  412.8 0.3 copy-done.9
  413.2 1.0 fusion.68
  414.2 0.2 copy-done.4
  414.4 0.3 copy-done.5
  414.7 1.0 fusion.59
  415.7 0.3 pad_maximum_fusion
  416.0 3.0 reshape.210
  419.0 6.8 %copy.75 = f32[64,2,3,2048]{3,1,2,0:T(2,128)} copy(f32[64,2,3,2048]{3,2,1,0:T(4,128)} %reshape.210) | data formatting | bytes 6291456 | tf_op jit(solution)/shard_map/reshape | solution.py:119
  (65 shorter events, 1.0 us)
Async XLA Ops:
  0.0 7.5 %copy-start.10 = (bf16[8,8,8,128]{3,2,1,0:T(8,128)(2,1)S(1)}, bf16[8,8,8,128]{3,2,1,0:T(8,128)(2,1)}, u32[]{:S(2)}) copy-start(bf16[8,8,8,128]{3,2,1,0:T(8,128)(2,1)} %param.13) | copy-start | bytes 393220
  0.0 7.5 %copy-start.13 = (f32[8,4,3]{0,1,2:T(4,128)S(1)}, f32[8,4,3]{0,1,2:T(4,128)}, u32[]{:S(2)}) copy-start(f32[8,4,3]{0,1,2:T(4,128)} %param.15) | copy-start | bytes 1156
  0.0 7.6 %copy-start.15 = (f32[8,4]{0,1:T(4,128)S(1)}, f32[8,4]{0,1:T(4,128)}, u32[]{:S(2)}) copy-start(f32[8,4]{0,1:T(4,128)} %param.16) | copy-start | bytes 388
  0.0 9.8 %copy-start.11 = (s32[8]{0:T(128)S(1)}, s32[8]{0:T(128)}, u32[]{:S(2)}) copy-start(s32[8]{0:T(128)} %param.19) | copy-start | bytes 100
  0.0 15.7 %copy-start.16 = (s32[8]{0:T(128)S(1)}, s32[8]{0:T(128)}, u32[]{:S(2)}) copy-start(s32[8]{0:T(128)} %param.20) | copy-start | bytes 100
  0.0 16.4 %copy-start.14 = (f32[8,16]{1,0:T(8,128)S(1)}, f32[8,16]{1,0:T(8,128)}, u32[]{:S(2)}) copy-start(f32[8,16]{1,0:T(8,128)} %param.17) | copy-start | bytes 1540
  0.0 78.1 %all-to-all-start = ((bf16[1,1024,2,3,2,128]{5,4,3,2,0,1:T(2,128)(2,1)}), bf16[1,1024,2,3,2,128]{5,4,3,2,0,1:T(2,128)(2,1)S(1)}, u32[]{:S(2)}, u32[]{:S(2)}) async-start(bf16[1,1024,2,3,2,128]{5,4,3,2,0,1:T(2,128)(2,1)} %bitcast.80), calls=%async_computation | async-start | bytes 6291456 | tf_op jit(solution)/shard_map/all_to_all | solution.py:46
  78.2 1.6 copy-start.2
  79.8 2.8 copy-start
  79.8 2.8 copy-start.1
  79.8 2.8 copy-start.3
  357.7 2.4 copy-start.12
  365.3 41.1 %all-to-all-start.1 = ((bf16[512,2,3,2,128]{4,3,2,1,0:T(2,128)(2,1)}), bf16[512,2,3,2,128]{4,3,2,1,0:T(2,128)(2,1)S(1)}, u32[]{:S(2)}, u32[]{:S(2)}) async-start(bf16[512,2,3,2,128]{4,3,2,1,0:T(2,128)(2,1)} %copy.73), calls=%async_computation.1 | async-start | bytes 3145728 | tf_op jit(solution)/shard_map/all_to_all | solution.py:100
  408.9 2.7 copy-start.6
  408.9 2.7 copy-start.7
  411.6 1.2 copy-start.8
  411.6 1.5 copy-start.9
  413.1 1.2 copy-start.4
  413.2 1.5 copy-start.5
where the time goes:
time: 426 us
  other arithmetic  223 us (52%)
  local copies, waits for them, and re-layouts  75.7 us (18%)
  waiting for transfers between devices  61 us (14%)
  matrix products  52.3 us (12%)
  starting transfers between devices  11.1 us (3%)
    another operation x6, other arithmetic  120 us
    cos x2, other arithmetic, one_turn(): wave_re = jnp.cos(phases)[:, :, :, None, None, :]  63.9 us
    all_to_all x1, waiting for transfers between devices, on_device(): lax.all_to_all(green, 'freq', split_axis=1, concat_axis=0, tiled=True)  61 us
    dot_general x2, matrix products, one_turn(): jnp.einsum('rgkp,ghfscqp->rkhfscq', routed, weighted, preferred_element_t...  46.6 us
    convert_element_type x2, other arithmetic, one_turn(): tile = tiles_here[region_map[blocks]].astype(jnp.float32)  28.8 us
    mul x2, local copies, waits for them, and re-layouts, one_turn(): wave_re * tile_re - wave_im * tile_im  28.4 us
    gather x4, local copies, waits for them, and re-layouts, one_turn(): tile = tiles_here[region_map[blocks]].astype(jnp.float32)  15 us
    reshape x2, local copies, waits for them, and re-layouts, on_device(): return motion.reshape(row_count, site_count, C, wave_len)  9.76 us
  transfers between devices with their start and end apart: 2, of which 1 were waited for; matrix products, arithmetic and copies ran while one was open for 11% of the time, Pallas kernels for 0%

commit v1 on v0

--- a/solution.py
+++ b/solution.py
@@ -8,6 +8,17 @@
 C = 3
 TWO_PI = 2.0 * math.pi
 OUT_GAIN = 8.0
+
+
+def refer_the_teams(inputs, axis_no, body):
+    s_next, a_next = (inputs.shape[:axis_no], inputs.shape[axis_no + 1 :])
+    return jnp.moveaxis(inputs.reshape(*s_next, body, -1, *a_next), axis_no, 0)
+
+
+def prepare_the_case(a0, dim_i):
+    d_next = list(a0.shape[1:])
+    d_next[dim_i] *= a0.shape[0]
+    return jnp.moveaxis(a0, 0, dim_i).reshape(d_next)
 
 
 def on_device(
@@ -43,7 +54,20 @@
     group_size = math.gcd(slot_total, 32)
     turn_count = slot_total // group_size
     rupture_ids = jnp.arange(rupture_count, dtype=jnp.int32)
-    tiles_here = lax.all_to_all(green, "freq", split_axis=1, concat_axis=0, tiled=True)
+    work_now, p_next = (lax.psum(1, "freq"), lax.axis_index("freq"))
+    t1 = refer_the_teams(green, 1, work_now)
+    panels = [t1[p_next]]
+    num = 1
+    while num < work_now:
+        outcome_arr = t1[(p_next + num) % work_now]
+        panels.append(
+            lax.ppermute(
+                outcome_arr, "freq", [(pp, (pp + num) % work_now) for pp in range(work_now)]
+            )
+        )
+        num = num + 1
+    t1 = jnp.stack(panels, axis=0)[(p_next - jnp.arange(work_now)) % work_now]
+    tiles_here = prepare_the_case(t1, 0)
     site_items = tiles_here.shape[2]
 
     def one_turn(turn_index, totals):

time: 426 us -> 429 us (level)
  waiting for transfers between devices: 61 us -> 24.9 us
  starting transfers between devices: 11.1 us -> 39.7 us
  local copies, waits for them, and re-layouts: 75.7 us -> 85.1 us
    all_to_all x1 -> x0, waiting for transfers between devices: 61 us -> none  [on_device(): lax.all_to_all(green, 'freq', split_axis=1, concat_axis=0, tiled=True)]
    ppermute x0 -> x7, waiting for transfers between devices: none -> 24.9 us  [on_device(): lax.ppermute(outcome_arr, 'freq', [(pp, (pp + num) % work_now) for pp in...]
    all_to_all x1, starting transfers between devices: 3.64 us -> 24.5 us  [on_device(): lax.all_to_all(spectrum, 'freq', split_axis=0, concat_axis=4, tiled=True)]
    ppermute x0 -> x7, starting transfers between devices: none -> 15.2 us  [on_device(): lax.ppermute(outcome_arr, 'freq', [(pp, (pp + num) % work_now) for pp in...]
    all_to_all x1 -> x0, starting transfers between devices: 7.44 us -> none  [on_device(): lax.all_to_all(green, 'freq', split_axis=1, concat_axis=0, tiled=True)]
    unnamed x38 -> x45, local copies, waits for them, and re-layouts: 5.76 us -> 10.7 us
  transfers between devices with their start and end apart: 2 -> 8, of which waited for: 1 -> 2; matrix products, arithmetic and copies ran while one was open for 11% -> 12% of each run, Pallas kernels for 0% -> 0%
where the time goes in v1:
time: 429 us; the launch traced here: 428 us
  other arithmetic  223 us (52%)
  local copies, waits for them, and re-layouts  85.1 us (20%)
  matrix products  52.3 us (12%)
  starting transfers between devices  39.7 us (9%)
  waiting for transfers between devices  24.9 us (6%)
    another operation x6, other arithmetic  120 us
    cos x2, other arithmetic, one_turn(): wave_re = jnp.cos(phases)[:, :, :, None, None, :]  63.9 us
    dot_general x2, matrix products, one_turn(): jnp.einsum('rgkp,ghfscqp->rkhfscq', routed, weighted, preferred_element_t...  46.6 us
    convert_element_type x2, other arithmetic, one_turn(): tile = tiles_here[region_map[blocks]].astype(jnp.float32)  28.9 us
    mul x2, local copies, waits for them, and re-layouts, one_turn(): wave_re * tile_re - wave_im * tile_im  28.3 us
    ppermute x7, waiting for transfers between devices, on_device(): lax.ppermute(outcome_arr, 'freq', [(pp, (pp + num) % work_now) for pp in...  24.9 us
    all_to_all x1, starting transfers between devices, on_device(): lax.all_to_all(spectrum, 'freq', split_axis=0, concat_axis=4, tiled=True)  24.5 us
    ppermute x7, starting transfers between devices, on_device(): lax.ppermute(outcome_arr, 'freq', [(pp, (pp + num) % work_now) for pp in...  15.2 us
  transfers between devices with their start and end apart: 8, of which 2 were waited for; matrix products, arithmetic and copies ran while one was open for 12% of the time, Pallas kernels for 0%

profile of v1, /device:TPU:0, one launch (start us, length us, event | category | flops | bytes accessed | tf_op | source)
XLA Modules:
  0.0 427.8 jit_solution(14357176411918231488)
XLA Ops:
  0.0 2.4 copy.75
  2.5 1.6 dynamic-slice_bitcast_fusion
  4.1 3.0 collective-permute-start
  7.0 1.6 collective-permute-start.1
  8.6 2.6 collective-permute-start.2
  11.2 1.2 collective-permute-start.3
  12.4 2.6 collective-permute-start.4
  15.1 0.7 fusion.82
  15.8 0.7 fusion.73
  16.6 5.1 %fusion.75 = pred[64]{0:T(512)(128)(4,1)S(1)} fusion(s32[]{:T(128)} %bitcast.2, s32[]{:T(128)} %bitcast.3, s32[]{:T(128)} %bitcast.4, s32[]{:T(128)} %bitcast.5, s32[]{:T(128)} %bitcast.6, s32[]{:T(128)} %bitcast.8, s32[]{:T(128)} %bitcast.7, s32[]{:T(128)} %bitcast.1), kind=kLoop, calls=%fused_computation.162 | loop fusion | flops 2048 | bytes 96 | tf_op jit(solution)/shard_map/lt | solution.py:53
  21.7 0.7 broadcast_compare_fusion
  22.4 2.1 all_gather.3
  24.7 1.4 collective-permute-start.5
  26.1 1.0 bitcast_dynamic-update-slice_fusion.7
  27.2 2.8 collective-permute-start.6
  30.0 1.0 bitcast_dynamic-update-slice_fusion.6
  31.1 22.3 %collective-permute-done.2 = bf16[1,128,2,3,2,128]{5,1,4,3,2,0:T(8,128)(2,1)} collective-permute-done((bf16[1,128,2,3,2,128]{5,1,4,3,2,0:T(8,128)(2,1)}, bf16[1,128,2,3,2,128]{5,1,4,3,2,0:T(8,128)(2,1)}, u32[]{:S(2)}, u32[]{:S(2)}) %collective-permute-start.2) | collective-permute-done | bytes 393248 | tf_op jit(solution)/shard_map/ppermute | solution.py:64
  53.4 1.0 bitcast_dynamic-update-slice_fusion.5
  54.4 1.0 bitcast_dynamic-update-slice_fusion.4
  55.5 1.0 bitcast_dynamic-update-slice_fusion.3
  56.6 2.6 collective-permute-done.6
  59.3 1.6 copy-done.2
  60.9 3.1 gather_fusion.7
  64.0 274.9 %while.14 = (s32[]{:T(128)}, f32[8,16,4,128,2,3,2]{3,1,6,5,4,2,0:T(8,128)}, s32[64]{0:T(128)S(1)}, pred[64]{0:T(512)(128)(4,1)S(1)}, s32[64]{0:T(128)S(1)}, /*in...) while((s32[]{:T(128)}, ...), condition=%wide.region_2.3_spmd.clone, body=%wide.region_0.2_spmd.clone.sunk | while | flops 6658150912 | bytes 280112832 | solution.py:105
  64.2 0.7 gather_fusion.1
  64.9 0.6 gather_fusion.2
  65.5 0.6 gather_fusion
  66.4 0.6 gather_fusion.3
  67.1 31.9 %multiply_cosine_fusion.2 = (f32[32,4,128,128]{3,2,0,1:T(8,128)}, f32[32,4,128,128]{3,2,0,1:T(8,128)}) fusion(f32[32,4,128]{2,0,1:T(8,128)S(1)} %sqrt_multiply_fusion.2, f32[128]{0:T(128)S(1)} %convert_multiply_fusion.3), kind=kLoop, calls=%fused_computation.17.clone.1 | loop fusion | flops 4194304 | bytes 16843264 | tf_op jit(solution)/shard_map/while/body/eval_jaxpr/cos | solution.py:86
  99.1 0.7 gather_fusion.4
  99.8 6.8 %gather_fusion.5 = bf16[32,128,2,3,2,128]{5,1,4,3,2,0:T(8,128)(2,1)} fusion(bf16[8,128,2,3,2,128]{5,1,4,3,2,0:T(8,128)(2,1)S(1)} %get-tuple-element.576, s32[1024]{0:T(1024)S(1)} %pad_clamp_fusion.9), kind=kCustom, calls=%fused_computation.6.clone.clone.1 | custom fusion | bytes 25165952 | tf_op jit(solution)/shard_map/while/body/eval_jaxpr/gather | solution.py:79
  106.6 14.5 %convert_element_type.116 = f32[32,128,2,3,2,128]{5,1,4,3,2,0:T(8,128)} convert(bf16[32,128,2,3,2,128]{5,1,4,3,2,0:T(8,128)(2,1)} %gather_fusion.5) | non-fusion elementwise | flops 6291456 | bytes 37748736 | tf_op jit(solution)/shard_map/while/body/eval_jaxpr/convert_element_type | solution.py:79
  121.1 14.2 %slice_bitcast_fusion.3 = (f32[32,128,2,3,128]{4,1,3,2,0:T(8,128)S(1)}, f32[32,128,2,3,128]{4,1,3,2,0:T(8,128)}) fusion(f32[32,128,2,3,2,128]{5,1,4,3,2,0:T(8,128)} %convert_element_type.116), kind=kLoop, calls=%fused_computation.15.clone.1 | loop fusion | bytes 50331648 | tf_op jit(solution)/shard_map/while/body/eval_jaxpr/mul | solution.py:91
  135.2 41.1 %subtract_convert_fusion.2 = (bf16[32,4,128,2,3,1,128]{6,2,0,5,4,3,1:T(8,128)(2,1)}, bf16[32,4,128,2,3,1,128]{6,2,0,5,4,3,1:T(8,128)(2,1)}) fusion(f32[32,4,128,128]{3,2,0,1:T(8,128)} %get-tuple-element.525, f32[32,4,128,128]{3,2,0,1:T(8,128)} %get-tuple-element.526, f32[32,128,2,3,128]{4,1,3,2,0:T(8,128)S(1)} %get-tuple-element.527, ...), kind=kLoop, calls=%fused_computation.12.clone.1 | loop fusion | flops 100663296 | bytes 92274688 | tf_op jit(solution)/shard_map/convert
  176.4 1.6 gather_fusion.6
  178.2 23.2 %bitcast_add_fusion.2 = f32[8,16,4,128,2,3,2]{3,1,6,5,4,2,0:T(8,128)} fusion(f32[8,16,4,128,2,3,2]{3,1,6,5,4,2,0:T(8,128)} %get-tuple-element.549, bf16[32,4,128,2,3,1,128]{6,2,0,5,4,3,1:T(8,128)(2,1)} %get-tuple-element.529, bf16[32,4,128,2,3,1,128]{6,2,0,5,4,3,1:T(8,128)(2,1)} %get-tuple-element.530, pred[]{:T(512)S(6)} %compare.117, ...), kind=kOutput, calls=%fused_computation.19.clone.1 | convolution fusion | flops 6546784256 | bytes 56754688 | tf_op jit(solution)/shard_map/while/body/eval_jaxpr/rgkp,ghfscqp->rkhfscq/dot_general | solution.py:97
  201.5 0.7 gather_fusion.1
  202.2 0.6 gather_fusion.2
  202.8 0.6 gather_fusion
  203.7 0.6 gather_fusion.3
  204.4 31.9 %multiply_cosine_fusion.2 = (f32[32,4,128,128]{3,2,0,1:T(8,128)}, f32[32,4,128,128]{3,2,0,1:T(8,128)}) fusion(f32[32,4,128]{2,0,1:T(8,128)S(1)} %sqrt_multiply_fusion.2, f32[128]{0:T(128)S(1)} %convert_multiply_fusion.3), kind=kLoop, calls=%fused_computation.17.clone.1 | loop fusion | flops 4194304 | bytes 16843264 | tf_op jit(solution)/shard_map/while/body/eval_jaxpr/cos | solution.py:86
  236.4 0.7 gather_fusion.4
  237.1 6.8 %gather_fusion.5 = bf16[32,128,2,3,2,128]{5,1,4,3,2,0:T(8,128)(2,1)} fusion(bf16[8,128,2,3,2,128]{5,1,4,3,2,0:T(8,128)(2,1)S(1)} %get-tuple-element.576, s32[1024]{0:T(1024)S(1)} %pad_clamp_fusion.9), kind=kCustom, calls=%fused_computation.6.clone.clone.1 | custom fusion | bytes 25165952 | tf_op jit(solution)/shard_map/while/body/eval_jaxpr/gather | solution.py:79
  243.9 14.5 %convert_element_type.116 = f32[32,128,2,3,2,128]{5,1,4,3,2,0:T(8,128)} convert(bf16[32,128,2,3,2,128]{5,1,4,3,2,0:T(8,128)(2,1)} %gather_fusion.5) | non-fusion elementwise | flops 6291456 | bytes 37748736 | tf_op jit(solution)/shard_map/while/body/eval_jaxpr/convert_element_type | solution.py:79
  258.3 14.2 %slice_bitcast_fusion.3 = (f32[32,128,2,3,128]{4,1,3,2,0:T(8,128)S(1)}, f32[32,128,2,3,128]{4,1,3,2,0:T(8,128)}) fusion(f32[32,128,2,3,2,128]{5,1,4,3,2,0:T(8,128)} %convert_element_type.116), kind=kLoop, calls=%fused_computation.15.clone.1 | loop fusion | bytes 50331648 | tf_op jit(solution)/shard_map/while/body/eval_jaxpr/mul | solution.py:91
  272.5 41.1 %subtract_convert_fusion.2 = (bf16[32,4,128,2,3,1,128]{6,2,0,5,4,3,1:T(8,128)(2,1)}, bf16[32,4,128,2,3,1,128]{6,2,0,5,4,3,1:T(8,128)(2,1)}) fusion(f32[32,4,128,128]{3,2,0,1:T(8,128)} %get-tuple-element.525, f32[32,4,128,128]{3,2,0,1:T(8,128)} %get-tuple-element.526, f32[32,128,2,3,128]{4,1,3,2,0:T(8,128)S(1)} %get-tuple-element.527, ...), kind=kLoop, calls=%fused_computation.12.clone.1 | loop fusion | flops 100663296 | bytes 92274688 | tf_op jit(solution)/shard_map/convert
  313.6 1.6 gather_fusion.6
  315.5 23.5 %bitcast_add_fusion.2 = f32[8,16,4,128,2,3,2]{3,1,6,5,4,2,0:T(8,128)} fusion(f32[8,16,4,128,2,3,2]{3,1,6,5,4,2,0:T(8,128)} %get-tuple-element.549, bf16[32,4,128,2,3,1,128]{6,2,0,5,4,3,1:T(8,128)(2,1)} %get-tuple-element.529, bf16[32,4,128,2,3,1,128]{6,2,0,5,4,3,1:T(8,128)(2,1)} %get-tuple-element.530, pred[]{:T(512)S(6)} %compare.117, ...), kind=kOutput, calls=%fused_computation.19.clone.1 | convolution fusion | flops 6546784256 | bytes 56754688 | tf_op jit(solution)/shard_map/while/body/eval_jaxpr/rgkp,ghfscqp->rkhfscq/dot_general | solution.py:97
  338.9 2.4 multiply_subtract_fusion
  341.7 2.0 copy.79
  343.7 2.8 copy.80
  346.5 24.5 %all-to-all-start = ((bf16[512,2,3,2,128]{4,3,2,1,0:T(2,128)(2,1)}), bf16[512,2,3,2,128]{4,3,2,1,0:T(2,128)(2,1)S(1)}, u32[]{:S(2)}, u32[]{:S(2)}) async-start(bf16[512,2,3,2,128]{4,3,2,1,0:T(2,128)(2,1)} %copy.80), calls=%async_computation | async-start | bytes 3145728 | tf_op jit(solution)/shard_map/all_to_all | solution.py:124
  371.0 9.3 %negate_convert_fusion.3 = (bf16[1024,512]{1,0:T(8,128)(2,1)}, bf16[1024,512]{1,0:T(8,128)(2,1)}) fusion(), kind=kLoop, calls=%fused_computation.98 | loop fusion | flops 8912896 | bytes 2097152 | tf_op jit(solution)/shard_map/convert.9
  380.3 9.4 %cosine_convert_fusion.1 = (bf16[1024,512]{1,0:T(8,128)(2,1)}, bf16[1024,512]{1,0:T(8,128)(2,1)}) fusion(s32[512]{0:T(512)S(1)} %iota_add_fusion.1), kind=kLoop, calls=%fused_computation.91 | loop fusion | flops 8912896 | bytes 2099200 | tf_op jit(solution)/shard_map/convert.4
  389.6 9.4 %cosine_convert_fusion.2 = (bf16[1024,512]{1,0:T(8,128)(2,1)}, bf16[1024,512]{1,0:T(8,128)(2,1)}) fusion(s32[512]{0:T(512)S(1)} %iota_add_fusion.2), kind=kLoop, calls=%fused_computation.95 | loop fusion | flops 8912896 | bytes 2099200 | tf_op jit(solution)/shard_map/convert.6
  399.0 9.3 %cosine_convert_fusion = (bf16[1024,512]{1,0:T(8,128)(2,1)}, bf16[1024,512]{1,0:T(8,128)(2,1)}) fusion(s32[512]{0:T(512)S(1)} %iota_add_fusion), kind=kLoop, calls=%fused_computation.87 | loop fusion | flops 8912896 | bytes 2099200 | tf_op jit(solution)/shard_map/convert.2
  408.3 1.8 copy.91
  410.2 0.7 reshape.259
  410.9 2.7 fusion.62
  413.6 1.0 fusion.65
  415.2 1.0 fusion.68
  416.7 1.0 fusion.59
  418.0 3.0 reshape.260
  421.0 6.8 %copy.82 = f32[64,2,3,2048]{3,1,2,0:T(2,128)} copy(f32[64,2,3,2048]{3,2,1,0:T(4,128)} %reshape.260) | data formatting | bytes 6291456 | tf_op jit(solution)/shard_map/reshape | solution.py:143
  (89 shorter events, 3.7 us)
Async XLA Ops:
  2.4 12.7 %copy-start.11 = (s32[8]{0:T(128)S(1)}, s32[8]{0:T(128)}, u32[]{:S(2)}) copy-start(s32[8]{0:T(128)} %param.19) | copy-start | bytes 100
  2.4 13.3 %copy-start.10 = (bf16[8,8,8,128]{3,2,1,0:T(8,128)(2,1)S(1)}, bf16[8,8,8,128]{3,2,1,0:T(8,128)(2,1)}, u32[]{:S(2)}) copy-start(bf16[8,8,8,128]{3,2,1,0:T(8,128)(2,1)} %param.13) | copy-start | bytes 393220
  2.5 13.4 %copy-start.14 = (f32[8,16]{1,0:T(8,128)S(1)}, f32[8,16]{1,0:T(8,128)}, u32[]{:S(2)}) copy-start(f32[8,16]{1,0:T(8,128)} %param.17) | copy-start | bytes 1540
  2.5 19.2 %copy-start.16 = (s32[8]{0:T(128)S(1)}, s32[8]{0:T(128)}, u32[]{:S(2)}) copy-start(s32[8]{0:T(128)} %param.20) | copy-start | bytes 100
  2.5 22.0 %copy-start.13 = (f32[8,4,3]{0,1,2:T(4,128)S(1)}, f32[8,4,3]{0,1,2:T(4,128)}, u32[]{:S(2)}) copy-start(f32[8,4,3]{0,1,2:T(4,128)} %param.15) | copy-start | bytes 1156
  2.5 22.1 %copy-start.15 = (f32[8,4]{0,1:T(4,128)S(1)}, f32[8,4]{0,1:T(4,128)}, u32[]{:S(2)}) copy-start(f32[8,4]{0,1:T(4,128)} %param.16) | copy-start | bytes 388
  4.1 20.7 %collective-permute-start = (bf16[1,128,2,3,2,128]{5,1,4,3,2,0:T(8,128)(2,1)}, bf16[1,128,2,3,2,128]{5,1,4,3,2,0:T(8,128)(2,1)}, u32[]{:S(2)}, u32[]{:S(2)}) collective-permute-start(bf16[1,128,2,3,2,128]{5,1,4,3,2,0:T(8,128)(2,1)} %get-tuple-element.415), channel_id=1, source_target_pairs={{0,2},{2,4},{4,6},{6,8},{8,10},{10,12},{12,14},{14,0},{1,3},{3,5},... | collective-permute-start | bytes 1179656 | tf_op jit(solution)/shard_map/ppermute | solution.py:64
  7.0 20.2 %collective-permute-start.1 = (bf16[1,128,2,3,2,128]{5,1,4,3,2,0:T(8,128)(2,1)}, bf16[1,128,2,3,2,128]{5,1,4,3,2,0:T(8,128)(2,1)}, u32[]{:S(2)}, u32[]{:S(2)}) collective-permute-start(bf16[1,128,2,3,2,128]{5,1,4,3,2,0:T(8,128)(2,1)} %get-tuple-element.414), channel_id=1, source_target_pairs={{0,4},{2,6},{4,8},{6,10},{8,12},{10,14},{12,0},{14,2},{1,5},{3,7},... | collective-permute-start | bytes 1179656 | tf_op jit(solution)/shard_map/ppermute | solution.py:64
  8.6 44.7 %collective-permute-start.2 = (bf16[1,128,2,3,2,128]{5,1,4,3,2,0:T(8,128)(2,1)}, bf16[1,128,2,3,2,128]{5,1,4,3,2,0:T(8,128)(2,1)}, u32[]{:S(2)}, u32[]{:S(2)}) collective-permute-start(bf16[1,128,2,3,2,128]{5,1,4,3,2,0:T(8,128)(2,1)} %get-tuple-element.413), channel_id=1, source_target_pairs={{0,6},{2,8},{4,10},{6,12},{8,14},{10,0},{12,2},{14,4},{1,7},{3,9},... | collective-permute-start | bytes 1179656 | tf_op jit(solution)/shard_map/ppermute | solution.py:64
  11.2 43.2 %collective-permute-start.3 = (bf16[1,128,2,3,2,128]{5,1,4,3,2,0:T(8,128)(2,1)}, bf16[1,128,2,3,2,128]{5,1,4,3,2,0:T(8,128)(2,1)}, u32[]{:S(2)}, u32[]{:S(2)}) collective-permute-start(bf16[1,128,2,3,2,128]{5,1,4,3,2,0:T(8,128)(2,1)} %get-tuple-element.412), channel_id=1, source_target_pairs={{0,8},{2,10},{4,12},{6,14},{8,0},{10,2},{12,4},{14,6},{1,9},{3,11}... | collective-permute-start | bytes 1179656 | tf_op jit(solution)/shard_map/ppermute | solution.py:64
  12.4 43.1 %collective-permute-start.4 = (bf16[1,128,2,3,2,128]{5,1,4,3,2,0:T(8,128)(2,1)}, bf16[1,128,2,3,2,128]{5,1,4,3,2,0:T(8,128)(2,1)}, u32[]{:S(2)}, u32[]{:S(2)}) collective-permute-start(bf16[1,128,2,3,2,128]{5,1,4,3,2,0:T(8,128)(2,1)} %get-tuple-element.411), channel_id=1, source_target_pairs={{0,10},{2,12},{4,14},{6,0},{8,2},{10,4},{12,6},{14,8},{1,11},{3,13... | collective-permute-start | bytes 1179656 | tf_op jit(solution)/shard_map/ppermute | solution.py:64
  24.7 31.8 %collective-permute-start.5 = (bf16[1,128,2,3,2,128]{5,1,4,3,2,0:T(8,128)(2,1)}, bf16[1,128,2,3,2,128]{5,1,4,3,2,0:T(8,128)(2,1)S(1)}, u32[]{:S(2)}, u32[]{:S(2)}) collective-permute-start(bf16[1,128,2,3,2,128]{5,1,4,3,2,0:T(8,128)(2,1)} %get-tuple-element.410), channel_id=1, source_target_pairs={{0,12},{2,14},{4,0},{6,2},{8,4},{10,6},{12,8},{14,10},{1,13},{3,15... | collective-permute-start | bytes 1179656 | tf_op jit(solution)/shard_map/ppermute | solution.py:64
  27.2 32.0 %collective-permute-start.6 = (bf16[1,128,2,3,2,128]{5,1,4,3,2,0:T(8,128)(2,1)}, bf16[1,128,2,3,2,128]{5,1,4,3,2,0:T(8,128)(2,1)S(1)}, u32[]{:S(2)}, u32[]{:S(2)}) collective-permute-start(bf16[1,128,2,3,2,128]{5,1,4,3,2,0:T(8,128)(2,1)} %get-tuple-element.409), channel_id=1, source_target_pairs={{0,14},{2,0},{4,2},{6,4},{8,6},{10,8},{12,10},{14,12},{1,15},{3,1}... | collective-permute-start | bytes 1179656 | tf_op jit(solution)/shard_map/ppermute | solution.py:64
  59.3 1.6 copy-start.2
  60.9 3.1 copy-start
  60.9 3.1 copy-start.1
  60.9 3.1 copy-start.3
  338.9 2.4 copy-start.12
  346.5 61.8 %all-to-all-start = ((bf16[512,2,3,2,128]{4,3,2,1,0:T(2,128)(2,1)}), bf16[512,2,3,2,128]{4,3,2,1,0:T(2,128)(2,1)S(1)}, u32[]{:S(2)}, u32[]{:S(2)}) async-start(bf16[512,2,3,2,128]{4,3,2,1,0:T(2,128)(2,1)} %copy.80), calls=%async_computation | async-start | bytes 3145728 | tf_op jit(solution)/shard_map/all_to_all | solution.py:124
  410.9 2.7 copy-start.6
  410.9 2.7 copy-start.7
  413.6 1.2 copy-start.8
  413.6 1.5 copy-start.9
  415.2 1.2 copy-start.4
  415.2 1.5 copy-start.5
